TPU v7x, 32 devices: a whole 2x2x4 slice. The times are simulated.
32 devices in a mesh: parts: 2 (over y), mp: 4 (over z), dp: 4 (over x, core).
Axes of the slice: x: 2, y: 2, z: 4, core: 2. Of those that a mesh axis runs over, the one named last changes fastest.
Arguments:
- embeddings: bfloat16 [2048, 1024], P(('parts', 'dp')), parts along dimension 0, may hold values from -16 to 16
- w_in: bfloat16 [1024, 8192], P(None, 'mp'), may hold values from -0.1875 to 0.1875
- w_out: bfloat16 [8192, 1024], P('mp'), may hold values from -0.0625 to 0.0625
- means: bfloat16 [8192, 1024], P('mp'), may hold values from -2.09375 to 2.09375
- precisions: bfloat16 [8192, 1024], P('mp'), may hold values from 0.04 to 0.16
- log_weight: float32 [8192], P('mp'), may hold values from -4 to 0
Outputs:
- counts: float32 [16384], P(('parts', 'mp')), parts along dimension 0
- first_moment: float32 [2048, 8192], P(('parts', 'dp'), 'mp'), parts along dimension 0
- second_moment: float32 [2048, 8192], P(('parts', 'dp'), 'mp'), parts along dimension 0
- grad_w_in: bfloat16 [2048, 8192], P(('parts', 'dp'), 'mp'), parts along dimension 0
- grad_w_out_t: bfloat16 [2048, 8192], P(('parts', 'dp'), 'mp'), parts along dimension 0
- grad_embed: bfloat16 [2048, 1024], P(('parts', 'dp')), parts along dimension 0
There are 2 independent parts, one for each index of `parts`. A program takes and returns all parts, laid end to end along the dimension named above; an argument that names none is the same for every part. Nothing has to cross between parts.
All inputs are finite; a program needn't handle non-finite values.
Results may differ from a plain program's by a relative error of at most 0.028.
Values may be sent and summed in bfloat16 or wider, within the bound.
A program may use at most 128 MiB of HBM per device.

v0:
```python
import jax
import jax.numpy as jnp
from jax import lax
from jax.sharding import PartitionSpec as P


def my_columns(rows, axis):
    gathered = lax.all_gather(rows, axis, axis=0, tiled=True)
    width = rows.shape[1] // lax.axis_size(axis)
    return lax.dynamic_slice_in_dim(gathered, lax.axis_index(axis) * width, width, 1)


def body(embeddings, w_in, w_out, means, precisions, log_weight):
    contract_rows = (((0,), (0,)), ((), ()))
    contract_cols = (((1,), (1,)), ((), ()))
    pre = jnp.dot(embeddings, w_in, preferred_element_type=jnp.float32)
    hidden = jax.nn.silu(pre).astype(jnp.bfloat16)
    hidden_all = lax.all_gather(hidden, "dp", axis=0, tiled=True)
    emb_cols = my_columns(embeddings, "dp")
    partial_value = jnp.dot(hidden, w_out, preferred_element_type=jnp.float32)
    head = lax.psum(partial_value, "mp").astype(jnp.bfloat16)
    head_f = head.astype(jnp.float32)
    squares = (head_f * head_f).astype(jnp.bfloat16)
    means_f = means.astype(jnp.float32)
    prec_f = precisions.astype(jnp.float32)
    weighted = (means_f * prec_f).astype(jnp.bfloat16)
    offset = (
        log_weight
        + 0.5 * jnp.sum(jnp.log(prec_f), axis=1)
        - 0.5 * jnp.sum(means_f * means_f * prec_f, axis=1)
    )
    scores = offset[None, :] + lax.dot_general(
        head, weighted, contract_cols, preferred_element_type=jnp.float32
    )
    scores = scores - 0.5 * lax.dot_general(
        squares, precisions, contract_cols, preferred_element_type=jnp.float32
    )
    local_top = jnp.max(scores, axis=1)
    local_total = jnp.sum(jnp.exp(scores - local_top[:, None]), axis=1)
    stats = lax.all_gather(jnp.stack([local_top, local_total]), "mp")
    top = jnp.max(stats[:, 0], axis=0)
    total = jnp.sum(stats[:, 1] * jnp.exp(stats[:, 0] - top), axis=0)
    lse = top + jnp.log(total)
    resp = jnp.exp(scores - lse[:, None])
    resp_b = resp.astype(jnp.bfloat16)
    counts = lax.psum(jnp.sum(resp, axis=0), "dp")
    resp_all = lax.all_gather(resp_b, "dp", axis=0, tiled=True)
    head_cols = my_columns(head, "dp")
    head_cols_f = head_cols.astype(jnp.float32)
    squares_cols = (head_cols_f * head_cols_f).astype(jnp.bfloat16)
    first_moment = lax.dot_general(
        head_cols, resp_all, contract_rows, preferred_element_type=jnp.float32
    )
    second_moment = lax.dot_general(
        squares_cols, resp_all, contract_rows, preferred_element_type=jnp.float32
    )
    along = jnp.dot(resp_b, precisions, preferred_element_type=jnp.float32)
    shifted = jnp.dot(resp_b, weighted, preferred_element_type=jnp.float32)
    grad_term = head_f * along - shifted
    grad_head = lax.psum(grad_term.astype(jnp.bfloat16), "mp")
    back = lax.dot_general(grad_head, w_out, contract_cols, preferred_element_type=jnp.float32)
    sigma = jax.nn.sigmoid(pre)
    grad_pre = (back * sigma * (1.0 + pre * (1.0 - sigma))).astype(jnp.bfloat16)
    embed_term = lax.dot_general(grad_pre, w_in, contract_cols, preferred_element_type=jnp.float32)
    grad_embed = lax.psum(embed_term.astype(jnp.bfloat16), "mp")
    pre_all = lax.all_gather(grad_pre, "dp", axis=0, tiled=True)
    grad_cols = my_columns(grad_head, "dp")
    grad_w_in = lax.dot_general(
        emb_cols, pre_all, contract_rows, preferred_element_type=jnp.float32
    ).astype(jnp.bfloat16)
    grad_w_out_t = lax.dot_general(
        grad_cols, hidden_all, contract_rows, preferred_element_type=jnp.float32
    ).astype(jnp.bfloat16)
    return (counts, first_moment, second_moment, grad_w_in, grad_w_out_t, grad_embed)


def solution(mesh):
    return jax.shard_map(
        body,
        mesh=mesh,
        in_specs=(
            P(("parts", "dp"), None),
            P(None, "mp"),
            P("mp", None),
            P("mp", None),
            P("mp", None),
            P("mp"),
        ),
        out_specs=(
            P(("parts", "mp")),
            P(("parts", "dp"), "mp"),
            P(("parts", "dp"), "mp"),
            P(("parts", "dp"), "mp"),
            P(("parts", "dp"), "mp"),
            P(("parts", "dp"), None),
        ),
        check_vma=False,
    )
```

profile of v0, /device:TPU:0, one launch (start us, length us, event | category | flops | bytes accessed | tf_op | source)
XLA Modules:
  0.0 288.4 jit_solution(5527400726379757286)
XLA Ops:
  8.0 5.0 %multiply_convert_fusion = (bf16[256,2048]{1,0:T(8,128)(2,1)S(1)}, f32[256,2048]{1,0:T(8,128)}) fusion(bf16[256,1024]{1,0:T(8,128)(2,1)} %param.6, bf16[1024,2048]{1,0:T(8,128)(2,1)} %param.7), kind=kOutput, calls=%fused_computation.17 | convolution fusion | flops 1076363264 | bytes 7864320 | tf_op jit(solution)/shard_map/dot_general | solution.py:16
  13.0 3.8 %fusion.34 = f32[256,1024]{1,0:T(8,128)S(1)} fusion(bf16[256,2048]{1,0:T(8,128)(2,1)S(1)} %get-tuple-element.13, bf16[2048,1024]{1,0:T(8,128)(2,1)} %param.8), kind=kOutput, calls=%fused_computation.50 | convolution fusion | flops 1073741824 | bytes 6291456 | tf_op jit(solution)/shard_map/dot_general | solution.py:20
  16.9 45.0 %all-reduce.7 = bf16[256,1024]{1,0:T(8,128)(2,1)S(1)} all-reduce(f32[256,1024]{1,0:T(8,128)S(1)} %fusion.34), channel_id=1, replica_groups=mesh['parts'=2,'mp'=4,'dp'=4] {'mp'}, use_global_device_ids=true, to_apply=%region_2.3 | all-reduce | flops 262144 | bytes 1572864 | tf_op jit(solution)/shard_map/psum | solution.py:21
  61.9 3.7 %convolution_multiply_fusion.1 = f32[256,2048]{1,0:T(8,128)S(1)} fusion(bf16[2048,1024]{1,0:T(8,128)(2,1)} %param.10, bf16[256,1024]{1,0:T(8,128)(2,1)S(1)} %all-reduce.7), kind=kOutput, calls=%fused_computation.8 | convolution fusion | flops 1075052544 | bytes 6815744 | tf_op jit(solution)/shard_map/dot_general | solution.py:35
  65.6 4.7 %fusion = (f32[2048]{0:T(1024)S(1)}, f32[2048]{0:T(1024)S(1)}) fusion(bf16[2048,1024]{1,0:T(8,128)(2,1)S(1)} %copy-done, bf16[2048,1024]{1,0:T(8,128)(2,1)} %param.9), kind=kLoop, calls=%fused_computation.4 | loop fusion | flops 12578816 | bytes 8404992 | tf_op jit(solution)/shard_map/reduce_sum | solution.py:29
  70.3 1.9 fusion.33
  72.7 11.9 %all-gather.1 = f32[4,2,256]{2,1,0:T(2,128)S(1)} all-gather(f32[1,2,256]{2,1,0:T(2,128)S(1)} %maximum_bitcast_fusion), channel_id=2, replica_groups=mesh['parts'=2,'mp'=4,'dp'=4] {'mp'}, dimensions={0}, use_global_device_ids=true | all-gather | bytes 10240 | tf_op jit(solution)/shard_map/all_gather | solution.py:40
  85.1 3.9 %convolution_multiply_fusion.2 = f32[256,1024]{1,0:T(8,128)S(1)} fusion(bf16[256,2048]{1,0:T(8,128)(2,1)S(1)} %get-tuple-element.8, bf16[2048,1024]{1,0:T(8,128)(2,1)} %param.10, bf16[256,1024]{1,0:T(8,128)(2,1)S(1)} %all-reduce.7), kind=kOutput, calls=%fused_computation.22 | convolution fusion | flops 1074266112 | bytes 6815744 | tf_op jit(solution)/shard_map/dot_general | solution.py:57
  89.0 4.6 %fusion.14 = bf16[256,1024]{1,0:T(8,128)(2,1)} fusion(f32[256,1024]{1,0:T(8,128)S(1)} %convolution_multiply_fusion.2, bf16[256,2048]{1,0:T(8,128)(2,1)S(1)} %get-tuple-element.8, bf16[2048,1024]{1,0:T(8,128)(2,1)S(1)} %copy-done.1, bf16[2048,1024]{1,0:T(8,128)(2,1)} %param.9), kind=kOutput, calls=%fused_computation.25 | convolution fusion | flops 1082654720 | bytes 11010048 | tf_op jit(solution)/shard_map/dot_general | solution.py:58
  94.9 36.3 %all-reduce.4.cloned.1.call-done = bf16[256,1024]{1,0:T(8,128)(2,1)} async-done(((bf16[256,1024]{1,0:T(8,128)(2,1)}), bf16[256,1024]{1,0:T(8,128)(2,1)}) %all-reduce.4.cloned.1.call-update) | async-done | bytes 524304 | tf_op jit(solution)/shard_map/psum | solution.py:60
  132.0 0.7 all-gather.13.cloned.1.call-update
  132.8 5.0 %fusion.5 = bf16[256,2048]{1,0:T(8,128)(2,1)} fusion(bf16[256,1024]{1,0:T(8,128)(2,1)} %all-reduce.4.cloned.1.call-done, bf16[2048,1024]{1,0:T(8,128)(2,1)} %param.8, f32[256,2048]{1,0:T(8,128)S(1)} %copy-done.8), kind=kOutput, calls=%fused_computation.12 | convolution fusion | flops 1078460416 | bytes 7864320 | tf_op jit(solution)/shard_map/dot_general | solution.py:61
  137.8 7.5 %psum.29 = f32[2048]{0:T(1024)} all-reduce(f32[2048]{0:T(1024)S(1)} %get-tuple-element.9), channel_id=1, replica_groups=mesh['parts'=2,'mp'=4,'dp'=4] {'dp'}, use_global_device_ids=true, to_apply=%region_8.9 | all-reduce | flops 2048 | bytes 16384 | tf_op jit(solution)/shard_map/psum | solution.py:46
  145.3 4.6 %convolution_convert_fusion.2 = bf16[256,1024]{1,0:T(8,128)(2,1)} fusion(bf16[256,2048]{1,0:T(8,128)(2,1)} %fusion.5, bf16[1024,2048]{1,0:T(8,128)(2,1)} %param.7), kind=kOutput, calls=%fused_computation.26 | convolution fusion | flops 1074003968 | bytes 5767168 | tf_op jit(solution)/shard_map/dot_general | solution.py:64
  150.0 4.2 %all-gather.11.cloned.1.call-done = bf16[1024,2048]{1,0:T(8,128)(2,1)} async-done(((bf16[256,2048]{1,0:T(8,128)(2,1)}), bf16[1024,2048]{1,0:T(8,128)(2,1)}) %all-gather.11.cloned.1.call-update) | async-done | bytes 4194320 | tf_op jit(solution)/shard_map/all_gather | solution.py:47
  154.2 5.2 %fusion.18 = f32[256,2048]{1,0:T(8,128)} fusion(bf16[1024,2048]{1,0:T(8,128)(2,1)} %all-gather.11.cloned.1.call-done, bf16[1024,1024]{1,0:T(8,128)(2,1)} %all-gather.9.cloned.1.call-done, s32[]{:T(128)S(6)} %select_n.2), kind=kOutput, calls=%fused_computation.29 | convolution fusion | flops 1074528256 | bytes 6815748 | tf_op jit(solution)/shard_map/dot_general | solution.py:54
  159.4 3.6 %fusion.23 = f32[256,2048]{1,0:T(8,128)} fusion(bf16[1024,2048]{1,0:T(8,128)(2,1)S(1)} %copy-done.7, bf16[1024,1024]{1,0:T(8,128)(2,1)} %all-gather.9.cloned.1.call-done, s32[]{:T(128)S(6)} %select_n.2), kind=kOutput, calls=%fused_computation.33 | convolution fusion | flops 1073741824 | bytes 6815748 | tf_op jit(solution)/shard_map/dot_general | solution.py:51
  163.0 15.1 %all-gather.17.cloned.1.call-done = bf16[1024,1024]{1,0:T(8,128)(2,1)} async-done(((bf16[256,1024]{1,0:T(8,128)(2,1)}), bf16[1024,1024]{1,0:T(8,128)(2,1)}) %all-gather.17.cloned.1.call-update) | async-done | bytes 2097168 | tf_op jit(solution)/shard_map/all_gather | solution.py:8
  178.0 35.9 %all-gather.19.cloned.1.call-done = bf16[1024,2048]{1,0:T(8,128)(2,1)} async-done(((bf16[256,2048]{1,0:T(8,128)(2,1)}), bf16[1024,2048]{1,0:T(8,128)(2,1)}) %all-gather.19.cloned.1.call-update) | async-done | bytes 4194320 | tf_op jit(solution)/shard_map/all_gather | solution.py:18
  214.0 4.6 %convolution_convert_fusion = bf16[256,2048]{1,0:T(8,128)(2,1)} fusion(bf16[1024,2048]{1,0:T(8,128)(2,1)} %all-gather.19.cloned.1.call-done, bf16[1024,1024]{1,0:T(8,128)(2,1)} %all-gather.17.cloned.1.call-done, s32[]{:T(128)S(6)} %select_n.2), kind=kOutput, calls=%fused_computation.13 | convolution fusion | flops 1074266112 | bytes 5767172 | tf_op jit(solution)/shard_map/dot_general | solution.py:71
  218.6 19.4 %all-gather.13.cloned.1.call-done = bf16[1024,1024]{1,0:T(8,128)(2,1)} async-done(((bf16[256,1024]{1,0:T(8,128)(2,1)}), bf16[1024,1024]{1,0:T(8,128)(2,1)}) %all-gather.13.cloned.1.call-update) | async-done | bytes 2097168 | tf_op jit(solution)/shard_map/all_gather | solution.py:8
  238.0 36.5 %all-gather.15.cloned.1.call-done = bf16[1024,2048]{1,0:T(8,128)(2,1)} async-done(((bf16[256,2048]{1,0:T(8,128)(2,1)}), bf16[1024,2048]{1,0:T(8,128)(2,1)}) %all-gather.15.cloned.1.call-update) | async-done | bytes 4194320 | tf_op jit(solution)/shard_map/all_gather | solution.py:66
  274.5 4.6 %convolution_convert_fusion.1 = bf16[256,2048]{1,0:T(8,128)(2,1)} fusion(bf16[1024,2048]{1,0:T(8,128)(2,1)} %all-gather.15.cloned.1.call-done, bf16[1024,1024]{1,0:T(8,128)(2,1)} %all-gather.13.cloned.1.call-done, s32[]{:T(128)S(6)} %select_n.2), kind=kOutput, calls=%fused_computation.14 | convolution fusion | flops 1074266112 | bytes 5767172 | tf_op jit(solution)/shard_map/dot_general | solution.py:68
  279.1 1.9 copy.26
  (42 shorter events, 3.1 us)
Async XLA Ops:
  8.0 123.2 %all-reduce.4.cloned.1.call-start = ((), (), s32[]{:S(2)}) async-start(), calls=%async_computation.3 | async-start | bytes 1048576 | tf_op jit(solution)/shard_map/psum | solution.py:60
  13.0 48.8 %copy-start.5 = (bf16[256,2048]{1,0:T(8,128)(2,1)}, bf16[256,2048]{1,0:T(8,128)(2,1)S(1)}, u32[]{:S(2)}) copy-start(bf16[256,2048]{1,0:T(8,128)(2,1)S(1)} %get-tuple-element.13) | copy-start | bytes 3145732
  61.9 23.2 %copy-start.4 = (bf16[256,1024]{1,0:T(8,128)(2,1)}, bf16[256,1024]{1,0:T(8,128)(2,1)S(1)}, u32[]{:S(2)}) copy-start(bf16[256,1024]{1,0:T(8,128)(2,1)S(1)} %all-reduce.7) | copy-start | bytes 1572868
  61.9 3.7 %copy-start = (bf16[2048,1024]{1,0:T(8,128)(2,1)S(1)}, bf16[2048,1024]{1,0:T(8,128)(2,1)}, u32[]{:S(2)}) copy-start(bf16[2048,1024]{1,0:T(8,128)(2,1)} %param.10) | copy-start | bytes 12582916
  65.6 4.7 %copy-start.6 = (f32[2048]{0:T(1024)S(1)}, f32[2048]{0:T(1024)}, u32[]{:S(2)}) copy-start(f32[2048]{0:T(1024)} %param.11) | copy-start | bytes 24580
  65.6 4.7 %copy-start.2 = (bf16[2048,1024]{1,0:T(8,128)(2,1)S(1)}, bf16[2048,1024]{1,0:T(8,128)(2,1)}, u32[]{:S(2)}) copy-start(bf16[2048,1024]{1,0:T(8,128)(2,1)} %param.9) | copy-start | bytes 12582916
  85.1 8.6 %copy-start.3 = (bf16[256,2048]{1,0:T(8,128)(2,1)}, bf16[256,2048]{1,0:T(8,128)(2,1)S(1)}, u32[]{:S(2)}) copy-start(bf16[256,2048]{1,0:T(8,128)(2,1)S(1)} %get-tuple-element.8) | copy-start | bytes 3145732
  85.1 3.9 %copy-start.1 = (bf16[2048,1024]{1,0:T(8,128)(2,1)S(1)}, bf16[2048,1024]{1,0:T(8,128)(2,1)}, u32[]{:S(2)}) copy-start(bf16[2048,1024]{1,0:T(8,128)(2,1)} %param.10) | copy-start | bytes 12582916
  93.6 39.1 %copy-start.8 = (f32[256,2048]{1,0:T(8,128)S(1)}, f32[256,2048]{1,0:T(8,128)}, u32[]{:S(2)}) copy-start(f32[256,2048]{1,0:T(8,128)} %get-tuple-element.14) | copy-start | bytes 6291460
  93.6 56.4 %all-gather.9.cloned.1.call-start = ((), (), s32[]{:S(2)}) async-start(), calls=%async_computation | async-start | bytes 2621440 | tf_op jit(solution)/shard_map/all_gather | solution.py:8
  94.2 59.9 %all-gather.11.cloned.1.call-start = ((), (), s32[]{:S(2)}) async-start(), calls=%async_computation.1 | async-start | bytes 5242880 | tf_op jit(solution)/shard_map/all_gather | solution.py:47
  94.8 83.2 %all-gather.17.cloned.1.call-start = ((), (), s32[]{:S(2)}) async-start(), calls=%async_computation.5 | async-start | bytes 2621440 | tf_op jit(solution)/shard_map/all_gather | solution.py:8
  131.2 82.8 %all-gather.19.cloned.1.call-start = ((), (), s32[]{:S(2)}) async-start(), calls=%async_computation.6 | async-start | bytes 5242880 | tf_op jit(solution)/shard_map/all_gather | solution.py:18
  132.0 106.1 %all-gather.13.cloned.1.call-start = ((), (), s32[]{:S(2)}) async-start(), calls=%async_computation.2 | async-start | bytes 2621440 | tf_op jit(solution)/shard_map/all_gather | solution.py:8
  132.7 141.8 %all-gather.15.cloned.1.call-start = ((), (), s32[]{:S(2)}) async-start(), calls=%async_computation.4 | async-start | bytes 5242880 | tf_op jit(solution)/shard_map/all_gather | solution.py:66
  137.8 141.4 %all-reduce.6.cloned.1.call-start = ((), (), s32[]{:S(2)}) async-start(), calls=%async_computation.7 | async-start | bytes 1048576 | tf_op jit(solution)/shard_map/psum | solution.py:65
  154.2 5.2 %copy-start.7 = (bf16[1024,2048]{1,0:T(8,128)(2,1)S(1)}, bf16[1024,2048]{1,0:T(8,128)(2,1)}, u32[]{:S(2)}) copy-start(bf16[1024,2048]{1,0:T(8,128)(2,1)} %all-gather.11.cloned.1.call-done) | copy-start | bytes 12582916
Sparse Core Ops, SparseCore 0:
  93.8 37.3 all-reduce.3
  150.1 38.3 all-reduce.5
Sparse Core Ops, SparseCore 1:
  96.3 21.2 all-gather.8
  119.5 34.6 all-gather.10
  155.6 22.4 all-gather.16
  179.6 34.3 all-gather.18
  215.6 22.4 all-gather.12
  240.2 34.3 all-gather.14
where the time goes:
time: 289 us; the launch traced here: 288 us
  waiting for transfers between devices  150 us (52%)
  blocking collectives  64.4 us (22%)
  matrix products  50.5 us (17%)
  between operations  15.8 us (5%)
  other arithmetic  5.57 us (2%)
    psum x1, blocking collectives, body(): head = lax.psum(partial_value, 'mp').astype(jnp.bfloat16)  45 us
    all_gather x1, waiting for transfers between devices, body(): pre_all = lax.all_gather(grad_pre, 'dp', axis=0, tiled=True)  36.5 us
    psum x1, waiting for transfers between devices, body(): grad_head = lax.psum(grad_term.astype(jnp.bfloat16), 'mp')  36.3 us
    all_gather x1, waiting for transfers between devices, body(): hidden_all = lax.all_gather(hidden, 'dp', axis=0, tiled=True)  35.9 us
    all_gather x3, waiting for transfers between devices, my_columns(): gathered = lax.all_gather(rows, axis, axis=0, tiled=True)  34.5 us
    all_gather x1, blocking collectives, body(): stats = lax.all_gather(jnp.stack([local_top, local_total]), 'mp')  11.9 us
    psum x1, blocking collectives, body(): counts = lax.psum(jnp.sum(resp, axis=0), 'dp')  7.52 us
  transfers between devices with their start and end apart: 8, of which 6 were waited for; matrix products, arithmetic and copies ran while one was open for 10% of the time, Pallas kernels for 0%

commit v1 on v0

--- a/solution.py
+++ b/solution.py
@@ -2,6 +2,7 @@
 import jax.numpy as jnp
 from jax import lax
 from jax.sharding import PartitionSpec as P
+from jax.lax import axis_index, axis_size, ppermute
 
 
 def my_columns(rows, axis):
@@ -63,7 +64,16 @@
     grad_pre = (back * sigma * (1.0 + pre * (1.0 - sigma))).astype(jnp.bfloat16)
     embed_term = lax.dot_general(grad_pre, w_in, contract_cols, preferred_element_type=jnp.float32)
     grad_embed = lax.psum(embed_term.astype(jnp.bfloat16), "mp")
-    pre_all = lax.all_gather(grad_pre, "dp", axis=0, tiled=True)
+    chips = axis_size("dp")
+    arr_out = sorted(((pp, (pp + 1) % chips) for pp in range(chips)))
+    d_next = grad_pre
+    xs_all = [d_next]
+    for dev_j in range(1, chips):
+        d_next = ppermute(d_next, axis_name="dp", perm=arr_out)
+        xs_all.insert(0, d_next)
+    res = jnp.concatenate(xs_all, 0)
+    block_last = axis_index("dp") + 1
+    pre_all = jnp.roll(res, block_last * grad_pre.shape[0], 0)
     grad_cols = my_columns(grad_head, "dp")
     grad_w_in = lax.dot_general(
         emb_cols, pre_all, contract_rows, preferred_element_type=jnp.float32

time: 289 us -> 264 us (0.913)
  waiting for transfers between devices: 150 us -> 106 us
  local copies, waits for them, and re-layouts: 1.92 us -> 13 us
  blocking collectives: 64.4 us -> 72.9 us
    ppermute x0 -> x3, waiting for transfers between devices: none -> 50.2 us  [body(): d_next = ppermute(d_next, axis_name='dp', perm=arr_out)]
    all_gather x1 -> x0, waiting for transfers between devices: 36.5 us -> none  [body(): pre_all = lax.all_gather(grad_pre, 'dp', axis=0, tiled=True)]
    all_gather x3, waiting for transfers between devices: 34.5 us -> 0.01 us  [my_columns(): gathered = lax.all_gather(rows, axis, axis=0, tiled=True)]
    all_gather x1, waiting for transfers between devices: 35.9 us -> 17.6 us  [body(): hidden_all = lax.all_gather(hidden, 'dp', axis=0, tiled=True)]
    unnamed x19 -> x26, local copies, waits for them, and re-layouts: 1.92 us -> 11.9 us
    psum x1, blocking collectives: 7.52 us -> 16 us  [body(): counts = lax.psum(jnp.sum(resp, axis=0), 'dp')]
    all_gather x1, waiting for transfers between devices: 4.16 us -> 0.01 us  [body(): resp_all = lax.all_gather(resp_b, 'dp', axis=0, tiled=True)]
  transfers between devices with their start and end apart: 8 -> 10, of which waited for: 6 -> 4; matrix products, arithmetic and copies ran while one was open for 10% -> 14% of each run, Pallas kernels for 0% -> 0%
where the time goes in v1:
time: 264 us
  waiting for transfers between devices  106 us (40%)
  blocking collectives  72.9 us (28%)
  matrix products  49.9 us (19%)
  between operations  15.9 us (6%)
  local copies, waits for them, and re-layouts  13 us (5%)
  other arithmetic  5.52 us (2%)
    ppermute x3, waiting for transfers between devices, body(): d_next = ppermute(d_next, axis_name='dp', perm=arr_out)  50.2 us
    psum x1, blocking collectives, body(): head = lax.psum(partial_value, 'mp').astype(jnp.bfloat16)  45 us
    psum x1, waiting for transfers between devices, body(): grad_head = lax.psum(grad_term.astype(jnp.bfloat16), 'mp')  35.8 us
    all_gather x1, waiting for transfers between devices, body(): hidden_all = lax.all_gather(hidden, 'dp', axis=0, tiled=True)  17.6 us
    psum x1, blocking collectives, body(): counts = lax.psum(jnp.sum(resp, axis=0), 'dp')  16 us
    unnamed x26, local copies, waits for them, and re-layouts  11.9 us
    all_gather x1, blocking collectives, body(): stats = lax.all_gather(jnp.stack([local_top, local_total]), 'mp')  11.9 us
    dot_general x1, matrix products, body(): lax.dot_general(squares_cols, resp_all, contract_rows, preferred_element_...  5.88 us
  transfers between devices with their start and end apart: 10, of which 4 were waited for; matrix products, arithmetic and copies ran while one was open for 14% of the time, Pallas kernels for 0%

profile of v1, /device:TPU:0, one launch (start us, length us, event | category | flops | bytes accessed | tf_op | source)
XLA Modules:
  0.0 263.7 jit_solution(9885129190286161165)
XLA Ops:
  8.0 5.0 %multiply_convert_fusion = (bf16[256,2048]{1,0:T(8,128)(2,1)S(1)}, f32[256,2048]{1,0:T(8,128)}) fusion(bf16[256,1024]{1,0:T(8,128)(2,1)} %param.6, bf16[1024,2048]{1,0:T(8,128)(2,1)} %param.7), kind=kOutput, calls=%fused_computation.19 | convolution fusion | flops 1076363264 | bytes 7864320 | tf_op jit(solution)/shard_map/dot_general | solution.py:17
  13.0 3.8 %fusion.39 = f32[256,1024]{1,0:T(8,128)S(1)} fusion(bf16[256,2048]{1,0:T(8,128)(2,1)S(1)} %get-tuple-element.13, bf16[2048,1024]{1,0:T(8,128)(2,1)} %param.8), kind=kOutput, calls=%fused_computation.60 | convolution fusion | flops 1073741824 | bytes 6291456 | tf_op jit(solution)/shard_map/dot_general | solution.py:21
  16.9 45.0 %all-reduce.7 = bf16[256,1024]{1,0:T(8,128)(2,1)S(1)} all-reduce(f32[256,1024]{1,0:T(8,128)S(1)} %fusion.39), channel_id=1, replica_groups=mesh['parts'=2,'mp'=4,'dp'=4] {'mp'}, use_global_device_ids=true, to_apply=%region_2.3 | all-reduce | flops 262144 | bytes 1572864 | tf_op jit(solution)/shard_map/psum | solution.py:22
  61.9 3.7 %convolution_multiply_fusion.1 = f32[256,2048]{1,0:T(8,128)S(1)} fusion(bf16[2048,1024]{1,0:T(8,128)(2,1)} %param.10, bf16[256,1024]{1,0:T(8,128)(2,1)S(1)} %all-reduce.7), kind=kOutput, calls=%fused_computation.10 | convolution fusion | flops 1075052544 | bytes 6815744 | tf_op jit(solution)/shard_map/dot_general | solution.py:36
  65.6 4.6 %fusion = (f32[2048]{0:T(1024)S(1)}, f32[2048]{0:T(1024)S(1)}) fusion(bf16[2048,1024]{1,0:T(8,128)(2,1)S(1)} %copy-done, bf16[2048,1024]{1,0:T(8,128)(2,1)} %param.9), kind=kLoop, calls=%fused_computation.4 | loop fusion | flops 12578816 | bytes 8404992 | tf_op jit(solution)/shard_map/reduce_sum | solution.py:30
  70.3 1.9 fusion.38
  72.6 11.9 %all-gather.1 = f32[4,2,256]{2,1,0:T(2,128)S(1)} all-gather(f32[1,2,256]{2,1,0:T(2,128)S(1)} %maximum_bitcast_fusion), channel_id=2, replica_groups=mesh['parts'=2,'mp'=4,'dp'=4] {'mp'}, dimensions={0}, use_global_device_ids=true | all-gather | bytes 10240 | tf_op jit(solution)/shard_map/all_gather | solution.py:41
  85.0 3.9 %convolution_multiply_fusion.2 = f32[256,1024]{1,0:T(8,128)S(1)} fusion(bf16[256,2048]{1,0:T(8,128)(2,1)S(1)} %get-tuple-element.8, bf16[2048,1024]{1,0:T(8,128)(2,1)} %param.10, bf16[256,1024]{1,0:T(8,128)(2,1)S(1)} %all-reduce.7), kind=kOutput, calls=%fused_computation.24 | convolution fusion | flops 1074266112 | bytes 6815744 | tf_op jit(solution)/shard_map/dot_general | solution.py:58
  89.0 4.6 %fusion.19 = bf16[256,1024]{1,0:T(8,128)(2,1)} fusion(f32[256,1024]{1,0:T(8,128)S(1)} %convolution_multiply_fusion.2, bf16[256,2048]{1,0:T(8,128)(2,1)S(1)} %get-tuple-element.8, bf16[2048,1024]{1,0:T(8,128)(2,1)S(1)} %copy-done.1, bf16[2048,1024]{1,0:T(8,128)(2,1)} %param.9), kind=kOutput, calls=%fused_computation.27 | convolution fusion | flops 1082654720 | bytes 11010048 | tf_op jit(solution)/shard_map/dot_general | solution.py:59
  95.4 35.8 %all-reduce.4.cloned.1.call-done = bf16[256,1024]{1,0:T(8,128)(2,1)} async-done(((bf16[256,1024]{1,0:T(8,128)(2,1)}), bf16[256,1024]{1,0:T(8,128)(2,1)}) %all-reduce.4.cloned.1.call-update) | async-done | bytes 524304 | tf_op jit(solution)/shard_map/psum | solution.py:61
  132.0 4.0 %fusion.10 = bf16[256,2048]{1,0:T(8,128)(2,1)S(1)} fusion(bf16[256,1024]{1,0:T(8,128)(2,1)} %all-reduce.4.cloned.1.call-done, bf16[2048,1024]{1,0:T(8,128)(2,1)} %param.8, f32[256,2048]{1,0:T(8,128)S(1)} %copy-done.8), kind=kOutput, calls=%fused_computation.15 | convolution fusion | flops 1078460416 | bytes 7864320 | tf_op jit(solution)/shard_map/dot_general | solution.py:62
  136.2 14.9 %collective-permute-done = bf16[256,2048]{1,0:T(8,128)(2,1)S(1)} collective-permute-done((bf16[256,2048]{1,0:T(8,128)(2,1)S(1)}, bf16[256,2048]{1,0:T(8,128)(2,1)S(1)}, u32[]{:S(2)}, u32[]{:S(2)}) %collective-permute-start) | collective-permute-done | bytes 1048608 | tf_op jit(solution)/shard_map/ppermute | solution.py:72
  151.1 35.3 %collective-permute-done.1 = bf16[256,2048]{1,0:T(8,128)(2,1)S(1)} collective-permute-done((bf16[256,2048]{1,0:T(8,128)(2,1)S(1)}, bf16[256,2048]{1,0:T(8,128)(2,1)S(1)}, u32[]{:S(2)}, u32[]{:S(2)}) %collective-permute-start.1) | collective-permute-done | bytes 1048608 | tf_op jit(solution)/shard_map/ppermute | solution.py:72
  186.5 16.0 %psum.29 = f32[2048]{0:T(1024)} all-reduce(f32[2048]{0:T(1024)S(1)} %get-tuple-element.9), channel_id=1, replica_groups=mesh['parts'=2,'mp'=4,'dp'=4] {'dp'}, use_global_device_ids=true, to_apply=%region_8.9 | all-reduce | flops 2048 | bytes 16384 | tf_op jit(solution)/shard_map/psum | solution.py:47
  202.5 4.3 %convolution_convert_fusion.1 = bf16[256,1024]{1,0:T(8,128)(2,1)} fusion(bf16[256,2048]{1,0:T(8,128)(2,1)S(1)} %fusion.10, bf16[1024,2048]{1,0:T(8,128)(2,1)} %param.7), kind=kOutput, calls=%fused_computation.28 | convolution fusion | flops 1074003968 | bytes 5767168 | tf_op jit(solution)/shard_map/dot_general | solution.py:65
  206.8 2.3 constant_dynamic-update-slice_fusion.7
  209.1 1.1 constant_dynamic-update-slice_fusion.6
  212.3 2.4 constant_dynamic-update-slice_fusion.3
  217.9 4.6 %fusion.7 = bf16[256,2048]{1,0:T(8,128)(2,1)} fusion(bf16[2048,2048]{1,0:T(8,128)(2,1)} %constant_dynamic-update-slice_fusion, s32[]{:T(128)S(6)} %select_n.20, bf16[1024,1024]{1,0:T(8,128)(2,1)} %all-gather.12.cloned.1.call-done, s32[]{:T(128)S(6)} %select_n.18), kind=kOutput, calls=%fused_computation.14 | convolution fusion | flops 1074266112 | bytes 5767176 | tf_op jit(solution)/shard_map/dot_general | solution.py:78
  222.5 5.9 %fusion.23 = f32[256,2048]{1,0:T(8,128)} fusion(bf16[1024,2048]{1,0:T(8,128)(2,1)} %all-gather.10.cloned.1.call-done, bf16[1024,1024]{1,0:T(8,128)(2,1)} %all-gather.8.cloned.1.call-done, s32[]{:T(128)S(6)} %select_n.18), kind=kOutput, calls=%fused_computation.31 | convolution fusion | flops 1074528256 | bytes 6815748 | tf_op jit(solution)/shard_map/dot_general | solution.py:55
  228.4 3.6 %fusion.28 = f32[256,2048]{1,0:T(8,128)} fusion(bf16[1024,2048]{1,0:T(8,128)(2,1)S(1)} %copy-done.7, bf16[1024,1024]{1,0:T(8,128)(2,1)} %all-gather.8.cloned.1.call-done, s32[]{:T(128)S(6)} %select_n.18), kind=kOutput, calls=%fused_computation.35 | convolution fusion | flops 1073741824 | bytes 6815748 | tf_op jit(solution)/shard_map/dot_general | solution.py:52
  232.1 17.6 %all-gather.16.cloned.1.call-done = bf16[1024,2048]{1,0:T(8,128)(2,1)} async-done(((bf16[256,2048]{1,0:T(8,128)(2,1)}), bf16[1024,2048]{1,0:T(8,128)(2,1)}) %all-gather.16.cloned.1.call-update) | async-done | bytes 4194320 | tf_op jit(solution)/shard_map/all_gather | solution.py:19
  249.6 4.6 %convolution_convert_fusion = bf16[256,2048]{1,0:T(8,128)(2,1)} fusion(bf16[1024,2048]{1,0:T(8,128)(2,1)} %all-gather.16.cloned.1.call-done, bf16[1024,1024]{1,0:T(8,128)(2,1)} %all-gather.14.cloned.1.call-done, s32[]{:T(128)S(6)} %select_n.18), kind=kOutput, calls=%fused_computation.16 | convolution fusion | flops 1074266112 | bytes 5767172 | tf_op jit(solution)/shard_map/dot_general | solution.py:81
  254.2 1.9 copy.33
  (53 shorter events, 9.1 us)
Async XLA Ops:
  8.0 123.1 %all-reduce.4.cloned.1.call-start = ((), (), s32[]{:S(2)}) async-start(), calls=%async_computation.3 | async-start | bytes 1048576 | tf_op jit(solution)/shard_map/psum | solution.py:61
  13.0 48.8 %copy-start.5 = (bf16[256,2048]{1,0:T(8,128)(2,1)}, bf16[256,2048]{1,0:T(8,128)(2,1)S(1)}, u32[]{:S(2)}) copy-start(bf16[256,2048]{1,0:T(8,128)(2,1)S(1)} %get-tuple-element.13) | copy-start | bytes 3145732
  61.9 23.2 %copy-start.4 = (bf16[256,1024]{1,0:T(8,128)(2,1)}, bf16[256,1024]{1,0:T(8,128)(2,1)S(1)}, u32[]{:S(2)}) copy-start(bf16[256,1024]{1,0:T(8,128)(2,1)S(1)} %all-reduce.7) | copy-start | bytes 1572868
  61.9 3.7 %copy-start = (bf16[2048,1024]{1,0:T(8,128)(2,1)S(1)}, bf16[2048,1024]{1,0:T(8,128)(2,1)}, u32[]{:S(2)}) copy-start(bf16[2048,1024]{1,0:T(8,128)(2,1)} %param.10) | copy-start | bytes 12582916
  65.6 4.6 %copy-start.6 = (f32[2048]{0:T(1024)S(1)}, f32[2048]{0:T(1024)}, u32[]{:S(2)}) copy-start(f32[2048]{0:T(1024)} %param.11) | copy-start | bytes 24580
  65.6 4.7 %copy-start.2 = (bf16[2048,1024]{1,0:T(8,128)(2,1)S(1)}, bf16[2048,1024]{1,0:T(8,128)(2,1)}, u32[]{:S(2)}) copy-start(bf16[2048,1024]{1,0:T(8,128)(2,1)} %param.9) | copy-start | bytes 12582916
  85.0 8.6 %copy-start.3 = (bf16[256,2048]{1,0:T(8,128)(2,1)}, bf16[256,2048]{1,0:T(8,128)(2,1)S(1)}, u32[]{:S(2)}) copy-start(bf16[256,2048]{1,0:T(8,128)(2,1)S(1)} %get-tuple-element.8) | copy-start | bytes 3145732
  85.0 3.9 %copy-start.1 = (bf16[2048,1024]{1,0:T(8,128)(2,1)S(1)}, bf16[2048,1024]{1,0:T(8,128)(2,1)}, u32[]{:S(2)}) copy-start(bf16[2048,1024]{1,0:T(8,128)(2,1)} %param.10) | copy-start | bytes 12582916
  93.6 38.4 %copy-start.8 = (f32[256,2048]{1,0:T(8,128)S(1)}, f32[256,2048]{1,0:T(8,128)}, u32[]{:S(2)}) copy-start(f32[256,2048]{1,0:T(8,128)} %get-tuple-element.14) | copy-start | bytes 6291460
  93.6 124.3 %all-gather.12.cloned.1.call-start = ((), (), s32[]{:S(2)}) async-start(), calls=%async_computation.2 | async-start | bytes 2621440 | tf_op jit(solution)/shard_map/all_gather | solution.py:9
  94.2 128.4 %all-gather.8.cloned.1.call-start = ((), (), s32[]{:S(2)}) async-start(), calls=%async_computation | async-start | bytes 2621440 | tf_op jit(solution)/shard_map/all_gather | solution.py:9
  94.8 127.8 %all-gather.10.cloned.1.call-start = ((), (), s32[]{:S(2)}) async-start(), calls=%async_computation.1 | async-start | bytes 5242880 | tf_op jit(solution)/shard_map/all_gather | solution.py:48
  95.3 136.7 %all-gather.14.cloned.1.call-start = ((), (), s32[]{:S(2)}) async-start(), calls=%async_computation.4 | async-start | bytes 2621440 | tf_op jit(solution)/shard_map/all_gather | solution.py:9
  131.2 118.4 %all-gather.16.cloned.1.call-start = ((), (), s32[]{:S(2)}) async-start(), calls=%async_computation.5 | async-start | bytes 5242880 | tf_op jit(solution)/shard_map/all_gather | solution.py:19
  131.9 122.3 %all-reduce.6.cloned.1.call-start = ((), (), s32[]{:S(2)}) async-start(), calls=%async_computation.6 | async-start | bytes 1048576 | tf_op jit(solution)/shard_map/psum | solution.py:66
  136.0 15.1 %collective-permute-start = (bf16[256,2048]{1,0:T(8,128)(2,1)S(1)}, bf16[256,2048]{1,0:T(8,128)(2,1)S(1)}, u32[]{:S(2)}, u32[]{:S(2)}) collective-permute-start(bf16[256,2048]{1,0:T(8,128)(2,1)S(1)} %fusion.10), channel_id=1, source_target_pairs={{0,1},{1,2},{2,3},{3,0},{4,5},{5,6},{6,7},{7,4},{8,9},{9,10},{10,1... | collective-permute-start | bytes 3145736 | tf_op jit(solution)/shard_map/ppermute | solution.py:72
  151.1 35.4 %collective-permute-start.1 = (bf16[256,2048]{1,0:T(8,128)(2,1)S(1)}, bf16[256,2048]{1,0:T(8,128)(2,1)S(1)}, u32[]{:S(2)}, u32[]{:S(2)}) collective-permute-start(bf16[256,2048]{1,0:T(8,128)(2,1)S(1)} %collective-permute-done), channel_id=1, source_target_pairs={{0,1},{1,2},{2,3},{3,0},{4,5},{5,6},{6,7},{7,4},{8,9},{9,10},{10,1... | collective-permute-start | bytes 3145736 | tf_op jit(solution)/shard_map/ppermute | solution.py:72
  186.5 20.3 %collective-permute-start.2 = (bf16[256,2048]{1,0:T(8,128)(2,1)S(1)}, bf16[256,2048]{1,0:T(8,128)(2,1)}, u32[]{:S(2)}, u32[]{:S(2)}) collective-permute-start(bf16[256,2048]{1,0:T(8,128)(2,1)S(1)} %collective-permute-done.1), channel_id=1, source_target_pairs={{0,1},{1,2},{2,3},{3,0},{4,5},{5,6},{6,7},{7,4},{8,9},{9,10},{10,1... | collective-permute-start | bytes 3145736 | tf_op jit(solution)/shard_map/ppermute | solution.py:72
  222.5 5.9 %copy-start.7 = (bf16[1024,2048]{1,0:T(8,128)(2,1)S(1)}, bf16[1024,2048]{1,0:T(8,128)(2,1)}, u32[]{:S(2)}) copy-start(bf16[1024,2048]{1,0:T(8,128)(2,1)} %all-gather.10.cloned.1.call-done) | copy-start | bytes 12582916
Sparse Core Ops, SparseCore 0:
  93.7 37.3 all-reduce.3
  206.9 39.6 all-reduce.5
Sparse Core Ops, SparseCore 1:
  95.6 21.2 all-gather.11
  118.9 22.9 all-gather.7
  143.9 45.5 all-gather.9
  191.0 22.7 all-gather.13
  215.3 34.3 all-gather.15
